TPU v7x, 512 devices: a whole 4x4x16 slice. The times are simulated.
512 devices in a mesh: grp: 4 (over x_lo, core), dp: 32 (over z, x_hi), mp: 4 (over y).
Axes of the slice: x: 4 (x_hi: 2, x_lo: 2; x = x_hi * 2 + x_lo), y: 4, z: 16, core: 2. Of those that a mesh axis runs over, the one named last changes fastest.
Arguments:
- neighbours: bfloat16 [512, 256, 896], P(('grp', 'dp')), may hold values from -6 to 6
- counts: int32 [512], P(('grp', 'dp')), may hold values from 0 to 2
- owner: int32 [512], P(('grp', 'dp')), may hold values from 0 to 511, as said below
- norm_gain: float32 [896], replicated, may hold values from 0.1 to 1.9
- w_in: bfloat16 [896, 3584], P('dp', 'mp'), may hold values from -0.1875 to 0.1875
- w_out: bfloat16 [3584, 896], P('mp', 'dp'), may hold values from -0.09375 to 0.09375
- w_key: bfloat16 [896, 4096], P('dp', 'mp'), may hold values from -0.1875 to 0.1875
- w_value: bfloat16 [896, 4096], P('dp', 'mp'), may hold values from -0.1875 to 0.1875
- queries: bfloat16 [32768, 4096], P(('grp', 'dp'), 'mp'), may hold values from -150 to 150
Outputs:
- attended: bfloat16 [32768, 4096], P(('grp', 'dp'), 'mp')
Inputs may be any that keep to these rules, and one draw needn't show every extreme that they name: owner is a permutation of the 512 query blocks. Span c stands on device c // 4 of grp+dp (index grp * 32 + dp); block owner[c] lies on device owner[c] // 4, which has the same dp index. Each device keeps 2 of its spans (their blocks lie on the device itself) and sends the other 2 to one other device along grp.
All inputs are finite; a program needn't handle non-finite values.
Results may differ from a plain program's by a relative error of at most 0.02.
Values may be sent and summed in bfloat16 or wider, within the bound.
A program may use at most 64 MiB of HBM per device.

v0:
```python
import jax
import jax.numpy as jnp
from jax import lax
from jax.sharding import PartitionSpec as P

HEAD = 128
NLEN = 128


def place_rows(received, meta, span_count):
    targets = jnp.arange(span_count, dtype=jnp.int32)[:, None]
    picker = meta[:, 0][None, :] == targets
    placed = jnp.einsum(
        "jb,btc->jtc", picker.astype(jnp.bfloat16), received, preferred_element_type=jnp.float32
    ).astype(jnp.bfloat16)
    live_counts = jnp.sum(jnp.where(picker, meta[:, 1][None, :], 0), axis=1).astype(jnp.int32)
    return (placed, live_counts)


def route_table(dest_grp, dest_slot, valid, extra, group_count, capacity):
    entries = dest_grp.shape[0]
    order = jnp.arange(entries, dtype=jnp.int32)
    earlier = (
        valid[None, :]
        & (dest_grp[None, :] == dest_grp[:, None])
        & (order[None, :] < order[:, None])
    )
    rank = jnp.sum(earlier.astype(jnp.int32), axis=1)
    bucket = jnp.where(valid, dest_grp * capacity + rank, -1)
    picker = bucket[None, :] == jnp.arange(group_count * capacity, dtype=jnp.int32)[:, None]
    slot_sent = jnp.sum(jnp.where(picker, dest_slot[None, :] + 1, 0), axis=1) - 1
    extra_sent = jnp.sum(jnp.where(picker, extra[None, :], 0), axis=1)
    meta = jnp.stack([slot_sent, extra_sent], axis=1)
    return (picker, meta)


def bucket_rows(rows, owner, extra, group_count, dp_count):
    span_count = owner.shape[0]
    dest_grp = owner // span_count // dp_count
    dest_slot = owner % span_count
    valid = jnp.ones((span_count,), dtype=bool)
    picker, meta = route_table(dest_grp, dest_slot, valid, extra, group_count, span_count // 2)
    packed = jnp.einsum(
        "bj,jtc->btc", picker.astype(jnp.bfloat16), rows, preferred_element_type=jnp.float32
    ).astype(jnp.bfloat16)
    return (packed, meta)


def attend_local(query_blocks, keys, values, live_counts):
    key_len = keys.shape[1]
    scores = jnp.einsum(
        "cqhd,ckhd->chqk", query_blocks, keys, preferred_element_type=jnp.float32
    ) * HEAD ** (-0.5)
    position = jnp.arange(key_len, dtype=jnp.int32) // NLEN
    live = (position[None, :] < live_counts[:, None])[:, None, None, :]
    masked = jnp.where(live, scores, -1e30)
    top = jnp.maximum(jnp.max(masked, axis=-1), 0.0)
    probs = jnp.where(live, jnp.exp(masked - top[..., None]), 0.0)
    denom = jnp.sum(probs, axis=-1) + jnp.exp(-top)
    weights = probs.astype(jnp.bfloat16)
    mixed = jnp.einsum("chqk,ckhd->cqhd", weights, values, preferred_element_type=jnp.float32)
    mixed = mixed / jnp.transpose(denom, (0, 2, 1))[..., None]
    span_count, span_len = (mixed.shape[0], mixed.shape[1])
    return mixed.astype(jnp.bfloat16).reshape(span_count, span_len, -1)


def on_device(neighbours, counts, owner, norm_gain, w_in, w_out, w_key, w_value, queries):
    span_count, key_len, enc_width = neighbours.shape
    group_count = lax.axis_size("grp")
    dp_count = lax.axis_size("dp")
    local_width = queries.shape[1]
    query_rows = queries.reshape(span_count, -1, local_width)
    flat = neighbours.astype(jnp.float32).reshape(-1, enc_width)
    meansq = jnp.mean(flat * flat, axis=-1, keepdims=True)
    normed = (flat * lax.rsqrt(meansq + 1e-06) * norm_gain).astype(jnp.bfloat16)
    columns = normed
    pre = jnp.dot(
        columns, lax.all_gather(w_in, "dp", axis=0, tiled=True), preferred_element_type=jnp.float32
    )
    hidden = jax.nn.gelu(pre, approximate=False).astype(jnp.bfloat16)
    partial_out = jnp.dot(
        hidden, lax.all_gather(w_out, "dp", axis=1, tiled=True), preferred_element_type=jnp.float32
    )
    total = lax.psum(partial_out, "mp")
    states = (flat + total).astype(jnp.bfloat16).reshape(span_count, key_len, enc_width)
    packed, meta = bucket_rows(states, owner, counts, group_count, dp_count)
    received, received_meta = (
        lax.all_to_all(packed, "grp", split_axis=0, concat_axis=0, tiled=True),
        lax.all_to_all(meta, "grp", split_axis=0, concat_axis=0, tiled=True),
    )
    served, live_counts = place_rows(received, received_meta, span_count)
    served_flat = served.reshape(-1, enc_width)
    columns = served_flat
    key_total = jnp.dot(
        columns, lax.all_gather(w_key, "dp", axis=0, tiled=True), preferred_element_type=jnp.float32
    )
    value_total = jnp.dot(
        columns,
        lax.all_gather(w_value, "dp", axis=0, tiled=True),
        preferred_element_type=jnp.float32,
    )
    heads = w_key.shape[1] // HEAD
    keys = key_total.astype(jnp.bfloat16).reshape(span_count, key_len, heads, HEAD)
    values = value_total.astype(jnp.bfloat16).reshape(span_count, key_len, heads, HEAD)
    query_blocks = query_rows.reshape(span_count, -1, heads, HEAD)
    mixed = attend_local(query_blocks, keys, values, live_counts)
    return mixed.reshape(queries.shape[0], queries.shape[1])


def solution(mesh):
    placed = (
        P(("grp", "dp"), None, None),
        P(("grp", "dp")),
        P(("grp", "dp")),
        P(),
        P("dp", "mp"),
        P("mp", "dp"),
        P("dp", "mp"),
        P("dp", "mp"),
        P(("grp", "dp"), "mp"),
    )
    return jax.shard_map(
        on_device, mesh=mesh, in_specs=placed, out_specs=P(("grp", "dp"), "mp"), check_vma=False
    )
```

profile of v0, /device:TPU:8, one launch (start us, length us, event | category | flops | bytes accessed | tf_op | source)
XLA Modules:
  0.0 746.3 jit_solution(8559613204974902349)
XLA Ops:
  6.5 0.0 all-gather.11.cloned.1.call-start
  6.5 0.7 all-gather.11.cloned.1.call-update
  7.3 0.0 all-gather.9.cloned.1.call-start
  7.3 0.7 all-gather.9.cloned.1.call-update
  8.0 0.0 all-reduce.2.cloned.1.call-start
  8.1 1.9 fusion.3
  10.0 2.0 fusion.5
  12.0 150.9 %all-gather.11.cloned.1.call-done = bf16[32,28,896]{2,1,0:T(8,128)(2,1)} async-done(((bf16[1,28,896]{2,1,0:T(8,128)(2,1)}), bf16[32,28,896]{2,1,0:T(8,128)(2,1)}) %all-gather.11.cloned.1.call-update) | async-done | bytes 1605648 | tf_op jit(solution)/shard_map/all_gather | solution.py:82
  162.9 2.4 reshape.107
  165.3 143.2 %all-gather.9.cloned.1.call-done = bf16[32,28,896]{2,1,0:T(8,128)(2,1)} async-done(((bf16[1,28,896]{2,1,0:T(8,128)(2,1)}), bf16[32,28,896]{2,1,0:T(8,128)(2,1)}) %all-gather.9.cloned.1.call-update) | async-done | bytes 1605648 | tf_op jit(solution)/shard_map/all_gather | solution.py:78
  308.5 3.5 reshape.105
  312.0 14.2 %fusion.23 = f32[1024,896]{1,0:T(8,128)} fusion(bf16[896,896]{1,0:T(8,128)(2,1)S(1)} %reshape.107, bf16[1024,896]{1,0:T(8,128)(2,1)S(1)} %fusion.5, bf16[896,896]{1,0:T(8,128)(2,1)} %reshape.105), kind=kOutput, calls=%fused_computation.41 | convolution fusion | flops 3347972096 | bytes 8716288 | tf_op jit(solution)/shard_map/dot_general | solution.py:81
  326.3 0.0 copy-start.4
  326.3 0.0 copy-start.3
  326.3 0.0 copy-start
  326.3 0.0 all-reduce.2.cloned.1.call-update
  326.3 0.0 all-gather.13.cloned.1.call-start
  326.3 0.5 all-gather.13.cloned.1.call-update
  326.9 0.0 all-gather.15.cloned.1.call-start
  326.9 0.5 all-gather.15.cloned.1.call-update
  327.5 0.0 copy-done.4
  327.5 0.2 convert_reduce_fusion
  327.7 0.0 copy-done.3
  327.7 0.1 select_reduce_fusion.2
  327.8 0.1 stack.7
  327.9 0.1 sub.29
  327.9 0.6 copy.28
  328.6 3.4 all-to-all-start
  332.0 87.4 %all-reduce.2.cloned.1.call-done = f32[1024,896]{1,0:T(8,128)} async-done(((f32[1024,896]{1,0:T(8,128)}), f32[1024,896]{1,0:T(8,128)}) %all-reduce.2.cloned.1.call-update) | async-done | bytes 3670032 | tf_op jit(solution)/shard_map/psum | solution.py:84
  419.4 0.0 copy-done
  419.4 2.4 fusion.6
  421.8 2.8 convolution_convert_fusion
  424.6 2.4 copy.31
  427.0 0.0 copy-start.2
  427.0 0.0 all-to-all-done
  427.0 4.9 all-to-all-start.1
  431.9 0.0 copy-done.2
  431.9 0.1 copy.40
  432.0 0.1 all_to_all.10
  432.1 0.1 select_reduce_fusion
  432.2 0.1 broadcast_compare_fusion
  432.3 141.0 %all-gather.13.cloned.1.call-done = bf16[32,28,1024]{2,1,0:T(8,128)(2,1)} async-done(((bf16[1,28,1024]{2,1,0:T(8,128)(2,1)}), bf16[32,28,1024]{2,1,0:T(8,128)(2,1)}) %all-gather.13.cloned.1.call-update) | async-done | bytes 1835024 | tf_op jit(solution)/shard_map/all_gather | solution.py:99
  573.3 2.5 reshape.109
  575.8 144.5 %all-gather.15.cloned.1.call-done = bf16[32,28,1024]{2,1,0:T(8,128)(2,1)} async-done(((bf16[1,28,1024]{2,1,0:T(8,128)(2,1)}), bf16[32,28,1024]{2,1,0:T(8,128)(2,1)}) %all-gather.15.cloned.1.call-update) | async-done | bytes 1835024 | tf_op jit(solution)/shard_map/all_gather | solution.py:95
  720.3 3.7 reshape.111
  724.1 0.0 all-to-all-done.1
  724.1 4.5 fusion.25
  728.5 0.2 copy.33
  728.8 2.4 convert_bitcast_fusion.1
  731.1 0.0 copy-start.1
  731.1 0.6 copy.41
  731.8 0.9 copy-done.1
  732.6 2.3 convert_bitcast_fusion
  734.9 0.6 copy.39
  735.6 0.9 bitcast_reduce_fusion
  736.5 0.9 fusion.28
  737.5 1.0 fusion.36
  738.5 0.3 copy.37
  738.8 0.9 copy.66
  (11 shorter events, 0.1 us)
Async XLA Ops:
  6.5 156.4 %all-gather.11.cloned.1.call-start = ((), (), s32[]{:S(2)}) async-start(), calls=%async_computation.4 | async-start | bytes 1892352 | tf_op jit(solution)/shard_map/all_gather | solution.py:82
  7.3 301.2 %all-gather.9.cloned.1.call-start = ((), (), s32[]{:S(2)}) async-start(), calls=%async_computation.3 | async-start | bytes 1892352 | tf_op jit(solution)/shard_map/all_gather | solution.py:78
  8.0 411.4 %all-reduce.2.cloned.1.call-start = ((), (), s32[]{:S(2)}) async-start(), calls=%async_computation.2 | async-start | bytes 7340032 | tf_op jit(solution)/shard_map/psum | solution.py:84
  326.3 1.2 copy-start.4
  326.3 1.4 copy-start.3
  326.3 93.1 %copy-start = (bf16[4,256,896]{2,1,0:T(8,128)(2,1)S(1)}, bf16[4,256,896]{2,1,0:T(8,128)(2,1)}, u32[]{:S(2)}) copy-start(bf16[4,256,896]{2,1,0:T(8,128)(2,1)} %param.9) | copy-start | bytes 5505028
  326.3 247.1 %all-gather.13.cloned.1.call-start = ((), (), s32[]{:S(2)}) async-start(), calls=%async_computation.5 | async-start | bytes 2162688 | tf_op jit(solution)/shard_map/all_gather | solution.py:99
  326.9 393.5 %all-gather.15.cloned.1.call-start = ((), (), s32[]{:S(2)}) async-start(), calls=%async_computation.6 | async-start | bytes 2162688 | tf_op jit(solution)/shard_map/all_gather | solution.py:95
  328.6 98.5 %all-to-all-start = ((s32[4,2,2]{1,2,0:T(2,128)}), s32[4,2,2]{1,2,0:T(2,128)S(1)}, u32[]{:S(2)}, u32[]{:S(2)}) async-start(s32[4,2,2]{1,2,0:T(2,128)} %copy.28), calls=%async_computation | async-start | bytes 8192 | tf_op jit(solution)/shard_map/all_to_all | solution.py:89
  427.0 4.9 copy-start.2
  427.0 297.0 %all-to-all-start.1 = ((bf16[8,256,896]{2,1,0:T(8,128)(2,1)}), bf16[8,256,896]{2,1,0:T(8,128)(2,1)}, u32[]{:S(2)}, u32[]{:S(2)}) async-start(bf16[8,256,896]{2,1,0:T(8,128)(2,1)} %copy.31), calls=%async_computation.1 | async-start | bytes 7340032 | tf_op jit(solution)/shard_map/all_to_all | solution.py:88
  731.1 1.5 copy-start.1
Sparse Core Ops, SparseCore 0:
  10.4 152.4 all-gather.10
  166.0 142.4 all-gather.8
  326.4 92.9 all-reduce.1
  422.3 150.9 all-gather.12
  576.3 144.0 all-gather.14
where the time goes:
time: 747 us; the launch traced here: 746 us
  waiting for transfers between devices  669 us (90%)
  matrix products  28.1 us (4%)
  local copies, waits for them, and re-layouts  19.1 us (3%)
  between operations  13.4 us (2%)
  starting transfers between devices  8.46 us (1%)
  other arithmetic  7.76 us (1%)
    all_gather x1, waiting for transfers between devices, on_device(): lax.all_gather(w_out, 'dp', axis=1, tiled=True)  151 us
    all_gather x1, waiting for transfers between devices, on_device(): lax.all_gather(w_key, 'dp', axis=0, tiled=True)  145 us
    all_gather x1, waiting for transfers between devices, on_device(): lax.all_gather(w_in, 'dp', axis=0, tiled=True)  143 us
    all_gather x1, waiting for transfers between devices, on_device(): lax.all_gather(w_value, 'dp', axis=0, tiled=True)  141 us
    psum x1, waiting for transfers between devices, on_device(): total = lax.psum(partial_out, 'mp')  87.4 us
    unnamed x19, local copies, waits for them, and re-layouts  15.3 us
  transfers between devices with their start and end apart: 7, of which 5 were waited for; matrix products, arithmetic and copies ran while one was open for 3% of the time, Pallas kernels for 0%

commit v1 on v0

--- a/solution.py
+++ b/solution.py
@@ -81,7 +81,7 @@
     partial_out = jnp.dot(
         hidden, lax.all_gather(w_out, "dp", axis=1, tiled=True), preferred_element_type=jnp.float32
     )
-    total = lax.psum(partial_out, "mp")
+    total = jnp.sum(lax.all_gather(partial_out, "mp"), axis=0)
     states = (flat + total).astype(jnp.bfloat16).reshape(span_count, key_len, enc_width)
     packed, meta = bucket_rows(states, owner, counts, group_count, dp_count)
     received, received_meta = (

time: 747 us -> 792 us (1.060)
  waiting for transfers between devices: 669 us -> 707 us
  other arithmetic: 7.76 us -> 16.1 us
    all_gather x0 -> x1, waiting for transfers between devices: none -> 133 us  [on_device(): total = jnp.sum(lax.all_gather(partial_out, 'mp'), axis=0)]
    psum x1 -> x0, waiting for transfers between devices: 87.4 us -> none  [on_device(): total = lax.psum(partial_out, 'mp')]
    all_gather x1, waiting for transfers between devices: 141 us -> 133 us  [on_device(): lax.all_gather(w_value, 'dp', axis=0, tiled=True)]
    reduce_sum x0 -> x1, other arithmetic: none -> 8.28 us  [on_device(): total = jnp.sum(lax.all_gather(partial_out, 'mp'), axis=0)]
  transfers between devices with their start and end apart: 7 -> 7, of which waited for: 5 -> 5; matrix products, arithmetic and copies ran while one was open for 3% -> 4% of each run, Pallas kernels for 0% -> 0%
where the time goes in v1:
time: 792 us
  waiting for transfers between devices  707 us (89%)
  matrix products  28.1 us (4%)
  local copies, waits for them, and re-layouts  19.2 us (2%)
  other arithmetic  16.1 us (2%)
  between operations  13.4 us (2%)
  starting transfers between devices  8.46 us (1%)
    all_gather x1, waiting for transfers between devices, on_device(): lax.all_gather(w_out, 'dp', axis=1, tiled=True)  151 us
    all_gather x1, waiting for transfers between devices, on_device(): lax.all_gather(w_key, 'dp', axis=0, tiled=True)  145 us
    all_gather x1, waiting for transfers between devices, on_device(): lax.all_gather(w_in, 'dp', axis=0, tiled=True)  143 us
    all_gather x1, waiting for transfers between devices, on_device(): total = jnp.sum(lax.all_gather(partial_out, 'mp'), axis=0)  133 us
    all_gather x1, waiting for transfers between devices, on_device(): lax.all_gather(w_value, 'dp', axis=0, tiled=True)  133 us
  transfers between devices with their start and end apart: 7, of which 5 were waited for; matrix products, arithmetic and copies ran while one was open for 4% of the time, Pallas kernels for 0%

profile of v1, /device:TPU:8, one launch (start us, length us, event | category | flops | bytes accessed | tf_op | source)
XLA Modules:
  0.0 791.8 jit_solution(14676164460622676423)
XLA Ops:
  6.5 0.0 all-gather.15.cloned.1.call-start
  6.5 0.7 all-gather.15.cloned.1.call-update
  7.3 0.0 all-gather.13.cloned.1.call-start
  7.3 0.7 all-gather.13.cloned.1.call-update
  8.0 0.0 all-gather.11.cloned.1.call-start
  8.1 1.9 multiply_reduce_fusion
  10.0 2.0 fusion.4
  12.0 150.9 %all-gather.15.cloned.1.call-done = bf16[32,28,896]{2,1,0:T(8,128)(2,1)} async-done(((bf16[1,28,896]{2,1,0:T(8,128)(2,1)}), bf16[32,28,896]{2,1,0:T(8,128)(2,1)}) %all-gather.15.cloned.1.call-update) | async-done | bytes 1605648 | tf_op jit(solution)/shard_map/all_gather | solution.py:82
  162.9 2.4 reshape.106
  165.3 143.2 %all-gather.13.cloned.1.call-done = bf16[32,28,896]{2,1,0:T(8,128)(2,1)} async-done(((bf16[1,28,896]{2,1,0:T(8,128)(2,1)}), bf16[32,28,896]{2,1,0:T(8,128)(2,1)}) %all-gather.13.cloned.1.call-update) | async-done | bytes 1605648 | tf_op jit(solution)/shard_map/all_gather | solution.py:78
  308.5 3.6 reshape.104
  312.1 14.2 %fusion.21 = f32[1024,896]{1,0:T(8,128)} fusion(bf16[896,896]{1,0:T(8,128)(2,1)S(1)} %reshape.106, bf16[1024,896]{1,0:T(8,128)(2,1)S(1)} %fusion.4, bf16[896,896]{1,0:T(8,128)(2,1)} %reshape.104), kind=kOutput, calls=%fused_computation.39 | convolution fusion | flops 3347972096 | bytes 8716288 | tf_op jit(solution)/shard_map/dot_general | solution.py:81
  326.3 0.0 copy-start.4
  326.3 0.0 copy-start.3
  326.3 0.0 all-gather.11.cloned.1.call-update
  326.3 0.0 all-gather.17.cloned.1.call-start
  326.4 0.5 all-gather.17.cloned.1.call-update
  326.9 0.0 all-gather.19.cloned.1.call-start
  327.0 0.5 all-gather.19.cloned.1.call-update
  327.5 0.0 copy-done.4
  327.5 0.2 convert_reduce_fusion
  327.7 0.0 copy-done.3
  327.7 0.1 select_reduce_fusion.2
  327.8 0.1 stack.7
  327.9 0.1 sub.29
  328.0 0.6 copy.28
  328.6 3.4 all-to-all-start
  332.0 132.8 %all-gather.11.cloned.1.call-done = f32[4096,896]{1,0:T(8,128)} async-done(((f32[1024,896]{1,0:T(8,128)}), f32[4096,896]{1,0:T(8,128)}) %all-gather.11.cloned.1.call-update) | async-done | bytes 14680080 | tf_op jit(solution)/shard_map/all_gather | solution.py:84
  464.8 0.0 copy-start
  464.8 8.3 %reduce_sum.69 = f32[1024,896]{1,0:T(8,128)} reduce(f32[4,1024,896]{2,1,0:T(8,128)} %bitcast.73, f32[]{:T(128)} %constant.38.clone.1), dimensions={0}, to_apply=%region_4.5 | reduce | flops 2752512 | bytes 18350084 | tf_op jit(solution)/shard_map/reduce_sum | solution.py:84
  473.1 0.0 copy-done
  473.1 2.4 add_convert_fusion
  475.5 2.8 convolution_convert_fusion
  478.3 2.4 copy.31
  480.8 0.0 copy-start.2
  480.8 0.0 all-to-all-done
  480.8 4.9 all-to-all-start.1
  485.7 0.0 copy-done.2
  485.7 0.1 copy.40
  485.8 0.1 all_to_all.10
  485.9 0.1 select_reduce_fusion
  486.0 0.1 broadcast_compare_fusion
  486.1 132.7 %all-gather.17.cloned.1.call-done = bf16[32,28,1024]{2,1,0:T(8,128)(2,1)} async-done(((bf16[1,28,1024]{2,1,0:T(8,128)(2,1)}), bf16[32,28,1024]{2,1,0:T(8,128)(2,1)}) %all-gather.17.cloned.1.call-update) | async-done | bytes 1835024 | tf_op jit(solution)/shard_map/all_gather | solution.py:99
  618.8 2.5 reshape.108
  621.3 144.5 %all-gather.19.cloned.1.call-done = bf16[32,28,1024]{2,1,0:T(8,128)(2,1)} async-done(((bf16[1,28,1024]{2,1,0:T(8,128)(2,1)}), bf16[32,28,1024]{2,1,0:T(8,128)(2,1)}) %all-gather.19.cloned.1.call-update) | async-done | bytes 1835024 | tf_op jit(solution)/shard_map/all_gather | solution.py:95
  765.8 3.8 reshape.110
  769.6 0.0 all-to-all-done.1
  769.6 4.5 fusion.23
  774.0 0.2 copy.33
  774.3 2.4 convert_bitcast_fusion.1
  776.6 0.0 copy-start.1
  776.6 0.6 copy.41
  777.3 0.9 copy-done.1
  778.1 2.3 convert_bitcast_fusion
  780.5 0.6 copy.39
  781.1 0.9 bitcast_reduce_fusion
  782.0 0.9 fusion.26
  783.0 1.0 fusion.34
  784.0 0.3 copy.37
  784.3 0.9 copy.66
  (11 shorter events, 0.1 us)
Async XLA Ops:
  6.5 156.4 %all-gather.15.cloned.1.call-start = ((), (), s32[]{:S(2)}) async-start(), calls=%async_computation.4 | async-start | bytes 1892352 | tf_op jit(solution)/shard_map/all_gather | solution.py:82
  7.3 301.2 %all-gather.13.cloned.1.call-start = ((), (), s32[]{:S(2)}) async-start(), calls=%async_computation.3 | async-start | bytes 1892352 | tf_op jit(solution)/shard_map/all_gather | solution.py:78
  8.0 456.8 %all-gather.11.cloned.1.call-start = ((), (), s32[]{:S(2)}) async-start(), calls=%async_computation.2 | async-start | bytes 18350080 | tf_op jit(solution)/shard_map/all_gather | solution.py:84
  326.3 1.2 copy-start.4
  326.3 1.4 copy-start.3
  326.3 292.5 %all-gather.17.cloned.1.call-start = ((), (), s32[]{:S(2)}) async-start(), calls=%async_computation.5 | async-start | bytes 2162688 | tf_op jit(solution)/shard_map/all_gather | solution.py:99
  326.9 438.9 %all-gather.19.cloned.1.call-start = ((), (), s32[]{:S(2)}) async-start(), calls=%async_computation.6 | async-start | bytes 2162688 | tf_op jit(solution)/shard_map/all_gather | solution.py:95
  328.6 152.2 %all-to-all-start = ((s32[4,2,2]{1,2,0:T(2,128)}), s32[4,2,2]{1,2,0:T(2,128)S(1)}, u32[]{:S(2)}, u32[]{:S(2)}) async-start(s32[4,2,2]{1,2,0:T(2,128)} %copy.28), calls=%async_computation | async-start | bytes 8192 | tf_op jit(solution)/shard_map/all_to_all | solution.py:89
  464.8 8.3 %copy-start = (bf16[4,256,896]{2,1,0:T(8,128)(2,1)S(1)}, bf16[4,256,896]{2,1,0:T(8,128)(2,1)}, u32[]{:S(2)}) copy-start(bf16[4,256,896]{2,1,0:T(8,128)(2,1)} %param.9) | copy-start | bytes 5505028
  480.8 4.9 copy-start.2
  480.8 288.8 %all-to-all-start.1 = ((bf16[8,256,896]{2,1,0:T(8,128)(2,1)}), bf16[8,256,896]{2,1,0:T(8,128)(2,1)}, u32[]{:S(2)}, u32[]{:S(2)}) async-start(bf16[8,256,896]{2,1,0:T(8,128)(2,1)} %copy.31), calls=%async_computation.1 | async-start | bytes 7340032 | tf_op jit(solution)/shard_map/all_to_all | solution.py:88
  776.6 1.5 copy-start.1
Sparse Core Ops, SparseCore 0:
  10.4 152.4 all-gather.14
  166.0 142.4 all-gather.12
  326.5 138.3 all-gather.10
  467.8 150.9 all-gather.16
  621.8 144.0 all-gather.18
